TPU v7x, 256 devices: a whole 4x4x8 slice. The times are simulated.
256 devices in a mesh: row: 32 (over y_hi, z, core), col: 8 (over x, y_lo).
Axes of the slice: x: 4, y: 4 (y_hi: 2, y_lo: 2; y = y_hi * 2 + y_lo), z: 8, core: 2. Of those that a mesh axis runs over, the one named last changes fastest.
Arguments:
- tokens: bfloat16 [1024, 16384], P('row', 'col'), may hold values from -6 to 6
- cotangent: bfloat16 [1024, 16384], P('row', 'col'), may hold values from -6 to 6
- w_gate: bfloat16 [16384, 12288], P('col', 'row'), may hold values from -0.046875 to 0.046875
- w_up: bfloat16 [16384, 12288], P('col', 'row'), may hold values from -0.046875 to 0.046875
- w_down: bfloat16 [12288, 16384], P('row', 'col'), may hold values from -0.0546875 to 0.0546875
Outputs:
- grad_tokens: bfloat16 [1024, 16384], P('row', 'col')
- grad_w_gate: bfloat16 [16384, 12288], P('col', 'row')
- grad_w_up: bfloat16 [16384, 12288], P('col', 'row')
- grad_w_down: bfloat16 [12288, 16384], P('row', 'col')
All inputs are finite; a program needn't handle non-finite values.
Results may differ from a plain program's by a relative error of at most 0.005.
Values may be sent and summed in bfloat16 or wider, within the bound.
A program may use at most 128 MiB of HBM per device.

v0:
```python
import jax
import jax.numpy as jnp
from jax import lax
from jax.sharding import PartitionSpec as P


def contract_rows(left, right):
    return lax.dot_general(
        left, right, (((0,), (0,)), ((), ())), preferred_element_type=jnp.float32
    )


def contract_cols(left, right):
    return lax.dot_general(
        left, right, (((1,), (1,)), ((), ())), preferred_element_type=jnp.float32
    )


def swiglu_grads(stacked, width):
    gate_value = stacked[:, :width]
    up_value = stacked[:, width : 2 * width]
    grad_act = stacked[:, 2 * width :]
    sigmoid_gate = jax.nn.sigmoid(gate_value)
    silu_gate = gate_value * sigmoid_gate
    activation = (silu_gate * up_value).astype(jnp.bfloat16)
    grad_gate = (
        grad_act * up_value * sigmoid_gate * (1.0 + gate_value * (1.0 - sigmoid_gate))
    ).astype(jnp.bfloat16)
    grad_up = (grad_act * silu_gate).astype(jnp.bfloat16)
    return (grad_gate, grad_up, activation)


def local(tokens, cotangent, w_gate, w_up, w_down):
    width = w_gate.shape[1]
    whole_x, whole_dy = (
        lax.all_gather(tokens, "row", axis=0, tiled=True),
        lax.all_gather(cotangent, "row", axis=0, tiled=True),
    )
    shares = lax.psum_scatter(
        jnp.concatenate(
            [
                jnp.dot(whole_x, w_gate, preferred_element_type=jnp.float32),
                jnp.dot(whole_x, w_up, preferred_element_type=jnp.float32),
                contract_cols(whole_dy, w_down),
            ],
            axis=1,
        ),
        "col",
        scatter_dimension=0,
        tiled=True,
    )
    grad_gate, grad_up, activation = swiglu_grads(shares, width)
    grad_gate, grad_up, activation = (
        lax.all_gather(grad_gate, "col", axis=0, tiled=True),
        lax.all_gather(grad_up, "col", axis=0, tiled=True),
        lax.all_gather(activation, "col", axis=0, tiled=True),
    )
    grad_w_gate = contract_rows(whole_x, grad_gate).astype(jnp.bfloat16)
    grad_w_up = contract_rows(whole_x, grad_up).astype(jnp.bfloat16)
    grad_w_down = contract_rows(activation, whole_dy).astype(jnp.bfloat16)
    grad_tokens = lax.psum_scatter(
        contract_cols(grad_gate, w_gate) + contract_cols(grad_up, w_up),
        "row",
        scatter_dimension=0,
        tiled=True,
    ).astype(jnp.bfloat16)
    return (grad_tokens, grad_w_gate, grad_w_up, grad_w_down)


def solution(mesh):
    placed = (P("row", "col"), P("row", "col"), P("col", "row"), P("col", "row"), P("row", "col"))
    return jax.shard_map(
        local,
        mesh=mesh,
        in_specs=placed,
        out_specs=(P("row", "col"), P("col", "row"), P("col", "row"), P("row", "col")),
        check_vma=False,
    )
```

profile of v0, /device:TPU:98, one launch (start us, length us, event | category | flops | bytes accessed | tf_op | source)
XLA Modules:
  0.0 517.3 jit_solution(1912775527264851470)
XLA Ops:
  7.2 0.0 copy-start
  7.2 0.0 all-gather.3.cloned.1.call-start
  7.2 0.7 all-gather.3.cloned.1.call-update
  7.9 0.0 all-gather.5.cloned.1.call-start
  8.0 0.7 all-gather.5.cloned.1.call-update
  8.7 0.0 reduce-scatter.3.cloned.1.call-start
  8.7 90.1 %all-gather.3.cloned.1.call-done = bf16[1024,2048]{1,0:T(8,128)(2,1)} async-done(((bf16[32,2048]{1,0:T(8,128)(2,1)}), bf16[1024,2048]{1,0:T(8,128)(2,1)}) %all-gather.3.cloned.1.call-update) | async-done | bytes 4194320 | tf_op jit(solution)/shard_map/all_gather | solution.py:36
  98.8 0.0 copy-start.3
  98.8 4.6 fusion.4
  103.5 0.0 copy-done
  103.5 0.0 copy-done.3
  103.5 3.0 fusion.3
  106.5 78.6 %all-gather.5.cloned.1.call-done = bf16[1024,2048]{1,0:T(8,128)(2,1)} async-done(((bf16[32,2048]{1,0:T(8,128)(2,1)}), bf16[1024,2048]{1,0:T(8,128)(2,1)}) %all-gather.5.cloned.1.call-update) | async-done | bytes 4194320 | tf_op jit(solution)/shard_map/all_gather | solution.py:37
  185.1 0.0 copy-start.2
  185.1 4.6 fusion.5
  189.7 0.0 copy-done.2
  189.7 2.6 pad_maximum_fusion
  192.3 0.0 reduce-scatter.3.cloned.1.call-update
  192.3 0.0 reduce-scatter.5.cloned.1.call-start
  192.4 100.1 %reduce-scatter.3.cloned.1.call-done = f32[128,1152]{0,1:T(8,128)} async-done(((f32[1024,1152]{0,1:T(8,128)}), f32[128,1152]{0,1:T(8,128)}) %reduce-scatter.3.cloned.1.call-update) | async-done | bytes 589840 | tf_op jit(solution)/shard_map/reduce_scatter | solution.py:39
  292.5 1.2 multiply_convert_fusion
  293.7 27.2 %all_gather.17 = bf16[1024,384]{0,1:T(8,128)(2,1)S(1)} all-gather(bf16[128,384]{0,1:T(8,128)(2,1)S(1)} %get-tuple-element.9), channel_id=1, replica_groups=mesh['row'=32,'col'=8] {'col'}, dimensions={0}, use_global_device_ids=true | all-gather | bytes 884736 | tf_op jit(solution)/shard_map/all_gather | solution.py:54
  320.9 26.4 %all_gather.18 = bf16[1024,384]{0,1:T(8,128)(2,1)S(1)} all-gather(bf16[128,384]{0,1:T(8,128)(2,1)S(1)} %get-tuple-element.10), channel_id=1, replica_groups=mesh['row'=32,'col'=8] {'col'}, dimensions={0}, use_global_device_ids=true | all-gather | bytes 884736 | tf_op jit(solution)/shard_map/all_gather | solution.py:55
  347.3 0.0 copy-start.1
  347.3 2.4 fusion.6
  349.7 0.0 copy-done.1
  349.7 5.7 %convolution_add_fusion = f32[1024,2048]{1,0:T(8,128)} fusion(f32[1024,2048]{1,0:T(8,128)S(1)} %fusion.6, bf16[1024,384]{0,1:T(8,128)(2,1)S(1)} %all_gather.18, bf16[2048,384]{1,0:T(8,128)(2,1)S(1)} %copy-done.1), kind=kOutput, calls=%fused_computation.1 | convolution fusion | flops 1612709888 | bytes 19136512 | tf_op jit(solution)/shard_map/dot_general | solution.py:14
  355.4 0.0 reduce-scatter.5.cloned.1.call-update
  355.4 5.1 fusion
  360.5 2.6 copy.9
  363.1 5.1 fusion.1
  368.2 2.6 copy.10
  370.9 25.7 %all_gather.19 = bf16[1024,384]{0,1:T(8,128)(2,1)S(1)} all-gather(bf16[128,384]{0,1:T(8,128)(2,1)S(1)} %get-tuple-element.8), channel_id=1, replica_groups=mesh['row'=32,'col'=8] {'col'}, dimensions={0}, use_global_device_ids=true | all-gather | bytes 884736 | tf_op jit(solution)/shard_map/all_gather | solution.py:56
  396.6 5.2 %convolution_convert_fusion = bf16[384,2048]{1,0:T(8,128)(2,1)} fusion(bf16[1024,384]{0,1:T(8,128)(2,1)S(1)} %all_gather.19, bf16[1024,2048]{1,0:T(8,128)(2,1)} %all-gather.5.cloned.1.call-done), kind=kOutput, calls=%fused_computation.2 | convolution fusion | flops 1611399168 | bytes 6553600 | tf_op jit(solution)/shard_map/dot_general | solution.py:8
  401.8 107.4 %reduce-scatter.5.cloned.1.call-done = f32[32,2048]{1,0:T(8,128)} async-done(((f32[1024,2048]{1,0:T(8,128)}), f32[32,2048]{1,0:T(8,128)}) %reduce-scatter.5.cloned.1.call-update) | async-done | bytes 262160 | tf_op jit(solution)/shard_map/reduce_scatter | solution.py:61
  509.2 1.6 convert_element_type.29
Async XLA Ops:
  7.2 96.3 %copy-start = (bf16[2048,384]{1,0:T(8,128)(2,1)S(1)}, bf16[2048,384]{1,0:T(8,128)(2,1)}, u32[]{:S(2)}) copy-start(bf16[2048,384]{1,0:T(8,128)(2,1)} %param.7) | copy-start | bytes 4718596
  7.2 91.6 %all-gather.3.cloned.1.call-start = ((), (), s32[]{:S(2)}) async-start(), calls=%async_computation.2 | async-start | bytes 4325376 | tf_op jit(solution)/shard_map/all_gather | solution.py:36
  7.9 177.2 %all-gather.5.cloned.1.call-start = ((), (), s32[]{:S(2)}) async-start(), calls=%async_computation.3 | async-start | bytes 4325376 | tf_op jit(solution)/shard_map/all_gather | solution.py:37
  8.7 283.8 %reduce-scatter.3.cloned.1.call-start = ((), (), s32[]{:S(2)}) async-start(), calls=%async_computation.4 | async-start | bytes 5308416 | tf_op jit(solution)/shard_map/reduce_scatter | solution.py:39
  98.8 4.7 copy-start.3
  185.1 4.6 copy-start.2
  192.3 316.9 %reduce-scatter.5.cloned.1.call-start = ((), (), s32[]{:S(2)}) async-start(), calls=%async_computation.5 | async-start | bytes 8650752 | tf_op jit(solution)/shard_map/reduce_scatter | solution.py:61
  347.3 2.4 copy-start.1
Sparse Core Ops, SparseCore 0:
  10.8 87.9 all-gather.2
  101.6 83.4 all-gather.4
  192.4 99.9 reduce-scatter.2
  355.5 153.6 reduce-scatter.4
where the time goes:
time: 520 us; the launch traced here: 517 us
  waiting for transfers between devices  378 us (73%)
  blocking collectives  79.4 us (15%)
  matrix products  35.7 us (7%)
  between operations  13.8 us (3%)
  other arithmetic  5.43 us (1%)
  local copies, waits for them, and re-layouts  5.23 us (1%)
    reduce_scatter x1, waiting for transfers between devices, local(): lax.psum_scatter(contract_cols(grad_gate, w_gate) + contract_cols(grad_up...  107 us
    reduce_scatter x1, waiting for transfers between devices, local(): lax.psum_scatter(jnp.concatenate([jnp.dot(whole_x, w_gate, preferred_elem...  100 us
    all_gather x1, waiting for transfers between devices, local(): lax.all_gather(tokens, 'row', axis=0, tiled=True)  90.1 us
    all_gather x1, waiting for transfers between devices, local(): lax.all_gather(cotangent, 'row', axis=0, tiled=True)  78.6 us
    all_gather x1, blocking collectives, local(): lax.all_gather(grad_gate, 'col', axis=0, tiled=True)  27.2 us
    all_gather x1, blocking collectives, local(): lax.all_gather(grad_up, 'col', axis=0, tiled=True)  26.4 us
    all_gather x1, blocking collectives, local(): lax.all_gather(activation, 'col', axis=0, tiled=True)  25.7 us
    dot_general x3, matrix products, contract_rows(): lax.dot_general(left, right, (((0,), (0,)), ((), ())), preferred_element_...  15.5 us
  transfers between devices with their start and end apart: 4, of which 4 were waited for; matrix products, arithmetic and copies ran while one was open for 5% of the time, Pallas kernels for 0%

commit v1 on v0

v1 whole, which is shorter than its diff:
```python
import jax
import jax.numpy as jnp
from jax import lax
from jax.experimental import pallas as pl
from jax.experimental.pallas import tpu as pltpu
from jax.sharding import PartitionSpec as P

MESH = pl.DeviceIdType.MESH
F32 = jnp.float32
BF16 = jnp.bfloat16

ZN = 8
CN = 8
STEPS = 8
SUB = 64
BLK = 2 * SUB
PIECE = BLK // CN
FEAT = 2048
HID = 384
H3 = 3 * HID
TOK = 32


def dot_nn(a, b):
    return lax.dot_general(a, b, (((1,), (0,)), ((), ())), preferred_element_type=F32)


def dot_nt(a, b):
    return lax.dot_general(a, b, (((1,), (1,)), ((), ())), preferred_element_type=F32)


def dot_tn(a, b):
    return lax.dot_general(a, b, (((0,), (0,)), ((), ())), preferred_element_type=F32)


def kernel(
    x_ref, dy_ref, wg_ref, wu_ref, wd_ref,
    gt_ref, gwg_ref, gwu_ref, gwd_ref,
    t_own, xy, wgu, wd, pf, own, pb, rb, hid, gf, r1, s2, r2, s3, rd, acc, ogu, od,
    w_sem, t_sem, o_sem, ex_s, ex_r, ring_s, ring_r, sib_s, sib_r,
    b_s, b_r, c_s, c_r, d1_s, d1_r, d2_s, d2_r, d3_s, d3_r,
):
    row = lax.axis_index("row")
    col = lax.axis_index("col")
    yh, z, c = row // (2 * ZN), (row // 2) % ZN, row % 2

    def at(dz=0, dyh=0, dc=0):
        return (((yh + dyh) % 2) * (2 * ZN) + ((z + dz + ZN) % ZN) * 2 + (c + dc) % 2, col)

    def colpeer(r):
        return (row, (col + r) % CN)

    sib, partner, cross = at(dc=1), at(dyh=1), at(dyh=1, dc=1)

    loads = [
        pltpu.make_async_copy(wg_ref, wgu.at[:, pl.ds(0, HID)], w_sem.at[0]),
        pltpu.make_async_copy(wu_ref, wgu.at[:, pl.ds(HID, HID)], w_sem.at[1]),
        pltpu.make_async_copy(wd_ref, wd, w_sem.at[2]),
    ]
    for cp in loads:
        cp.start()

    barrier = pltpu.get_barrier_semaphore()
    greet = [sib, partner, cross]
    greet += [at(dz=k) for k in range(1, ZN)]
    greet += [colpeer(r) for r in range(1, CN)]
    for d in greet:
        pl.semaphore_signal(barrier, inc=1, device_id=d, device_id_type=MESH)
    t_own[0] = x_ref[...]
    t_own[1] = dy_ref[...]
    pl.semaphore_wait(barrier, len(greet))

    def remote(src, dst, ss, rs, dev):
        return pltpu.make_async_remote_copy(
            src_ref=src, dst_ref=dst, send_sem=ss, recv_sem=rs, device_id=dev, device_id_type=MESH
        )

    pending = []

    def go(cp):
        cp.start()
        pending.append(cp)
        return cp

    mine = pl.ds(pl.multiple_of(c * TOK, TOK), TOK)
    go(remote(t_own.at[1 - c], xy.at[1 - c, 0, 0, mine], ex_s.at[0], ex_r.at[0], sib))
    go(remote(t_own.at[c], xy.at[c, 0, 1, mine], ex_s.at[1], ex_r.at[1], partner))
    go(remote(t_own.at[1 - c], xy.at[1 - c, 0, 1, mine], ex_s.at[2], ex_r.at[2], cross))
    keep = pltpu.make_async_copy(t_own.at[c], xy.at[c, 0, 0, mine], t_sem)
    keep.start()

    theirs = pl.ds(pl.multiple_of((1 - c) * TOK, TOK), TOK)

    def arrived(src, dst, ss, rs):
        remote(src, dst, ss, rs, sib).wait_recv()

    nxt = (at(dz=1), at(dz=-1))

    def send_ring(src_step, src_half, dst_step, d):
        go(
            remote(
                xy.at[c, src_step, src_half], xy.at[c, dst_step, d],
                ring_s.at[dst_step - 1, d], ring_r.at[dst_step - 1, d], nxt[d],
            )
        )

    def stage_gather(s):
        if s == 0:
            keep.wait()
            arrived(t_own.at[0], xy.at[c, 0, 0, theirs], ex_s.at[0], ex_r.at[0])
            send_ring(0, 0, 1, 0)
            send_ring(0, 0, 1, 1)
            arrived(t_own.at[0], xy.at[c, 0, 1, mine], ex_s.at[1], ex_r.at[1])
            arrived(t_own.at[0], xy.at[c, 0, 1, theirs], ex_s.at[2], ex_r.at[2])
            send_ring(0, 1, 2, 0)
            send_ring(0, 1, 2, 1)
        else:
            for d in range(2):
                arrived(xy.at[c, s, d], xy.at[c, s, d], ring_s.at[s - 1, d], ring_r.at[s - 1, d])
                if s <= 4 or (s == 5 and d == 0) or (s == 6 and d == 1):
                    send_ring(s, d, 7 if s >= 5 else s + 2, d)
        go(remote(xy.at[c, s], xy.at[c, s], sib_s.at[s], sib_r.at[s], sib))

    me16 = pl.ds(pl.multiple_of(col * PIECE, PIECE), PIECE)

    def stage_forward(s):
        arrived(xy.at[1 - c, s], xy.at[1 - c, s], sib_s.at[s], sib_r.at[s])
        if s == 0:
            for cp in loads:
                cp.wait()
        pf[:, : 2 * HID] = dot_nn(xy[0, s].reshape(BLK, FEAT), wgu[...])
        pf[:, 2 * HID :] = dot_nt(xy[1, s].reshape(BLK, FEAT), wd[...])
        pb[s] = pf[...].astype(BF16)
        own[s] = pf[me16, :]
        for r in range(1, CN):
            q = (col + r) % CN
            go(
                remote(
                    pb.at[s, pl.ds(pl.multiple_of(q * PIECE, PIECE), PIECE)], rb.at[s, r - 1],
                    b_s.at[s, r - 1], b_r.at[s, r - 1], colpeer(r),
                )
            )

    def stage_hidden(s):
        total = own[s]
        for r in range(1, CN):
            arrived(rb.at[s, r - 1], rb.at[s, r - 1], b_s.at[s, r - 1], b_r.at[s, r - 1])
            total = total + rb[s, r - 1].astype(F32)
        gate_value = total[:, :HID]
        up_value = total[:, HID : 2 * HID]
        grad_act = total[:, 2 * HID :]
        sig = jax.nn.sigmoid(gate_value)
        silu = gate_value * sig
        hid[s, me16, pl.ds(0, HID)] = (
            grad_act * up_value * sig * (1.0 + gate_value * (1.0 - sig))
        ).astype(BF16)
        hid[s, me16, pl.ds(HID, HID)] = (grad_act * silu).astype(BF16)
        hid[s, me16, pl.ds(2 * HID, HID)] = (silu * up_value).astype(BF16)
        for r in range(1, CN):
            go(remote(hid.at[s, me16], hid.at[s, me16], c_s.at[s, r - 1], c_r.at[s, r - 1], colpeer(r)))

    def stage_tokens(s):
        for r in range(1, CN):
            q = (col - r + CN) % CN
            piece = hid.at[s, pl.ds(pl.multiple_of(q * PIECE, PIECE), PIECE)]
            arrived(piece, piece, c_s.at[s, r - 1], c_r.at[s, r - 1])
        gf[s] = dot_nt(hid[s, :, : 2 * HID], wgu[...]).reshape(2, 2, TOK, FEAT)
        for d in range(2):
            go(remote(gf.at[s, d, 1 - c], r1.at[s, d], d1_s.at[s, d], d1_r.at[s, d], sib))

    def stage_pair(s):
        for d in range(2):
            arrived(r1.at[s, d], r1.at[s, d], d1_s.at[s, d], d1_r.at[s, d])
        for d in range(2):
            v = gf[s, d, c] + r1[s, d]
            other = d == 1 if s in (0, 7) else s % 2 == 0
            if other:
                k = (s + 1) // 2
                s2[k, d] = v.astype(BF16)
                go(remote(s2.at[k, d], r2.at[k, d], d2_s.at[k, d], d2_r.at[k, d], partner))
            else:
                acc[(s + 1) // 2, d] = v

    def stage_home(k):
        for d in range(2):
            src = 1 if k in (0, 4) else d
            if k in (0, 4) and d == 1:
                continue
            arrived(r2.at[k, src], r2.at[k, src], d2_s.at[k, src], d2_r.at[k, src])
            v = acc[k, d] + r2[k, src].astype(F32)
            if k == 0:
                acc[0, 0] = v
            else:
                slot = 2 * (k - 1) + d
                s3[slot] = v.astype(BF16)
                dest = at(dz=k if d else -k)
                go(remote(s3.at[slot], rd.at[slot], d3_s.at[slot], d3_r.at[slot], dest))

    outs = []

    def weight_grads(which):
        hs = hid[...].reshape(STEPS * BLK, H3)
        if which < 2:
            for m in range(4):
                f = (which * 4 + m) * 256
                ogu[pl.ds(f, 256), :] = dot_tn(
                    xy[0, :, :, :, f : f + 256].reshape(STEPS * BLK, 256), hs[:, : 2 * HID]
                ).astype(BF16)
        else:
            for m in range(8):
                f = m * 256
                od[:, pl.ds(f, 256)] = dot_tn(
                    hs[:, 2 * HID :], xy[1, :, :, :, f : f + 256].reshape(STEPS * BLK, 256)
                ).astype(BF16)
        if which == 1:
            outs.append(pltpu.make_async_copy(ogu.at[:, pl.ds(0, HID)], gwg_ref, o_sem.at[0]))
            outs.append(pltpu.make_async_copy(ogu.at[:, pl.ds(HID, HID)], gwu_ref, o_sem.at[1]))
            outs[0].start()
            outs[1].start()
        if which == 2:
            outs.append(pltpu.make_async_copy(od, gwd_ref, o_sem.at[2]))
            outs[2].start()

    for i in range(STEPS + 4):
        if i < STEPS:
            stage_gather(i)
        if 0 <= i - 3 < STEPS:
            stage_pair(i - 3)
        if i < STEPS:
            stage_forward(i)
        if 0 <= i - 1 < STEPS:
            stage_hidden(i - 1)
        if 0 <= i - 2 < STEPS:
            stage_tokens(i - 2)
        j = i - 4
        if 0 <= j < STEPS and (j % 2 == 0 or j == 7):
            stage_home((j + 1) // 2)
        if i >= STEPS + 1:
            weight_grads(i - STEPS - 1)

    total = acc[0, 0]
    for slot in range(ZN - 1):
        arrived(rd.at[slot], rd.at[slot], d3_s.at[slot], d3_r.at[slot])
        total = total + rd[slot].astype(F32)
    gt_ref[...] = total.astype(BF16)
    for cp in pending:
        cp.wait_send()
    for cp in outs:
        cp.wait()


def local(tokens, cotangent, w_gate, w_up, w_down):
    dma = pltpu.SemaphoreType.DMA
    vm = pltpu.VMEM
    any_spec = pl.BlockSpec(memory_space=pl.ANY)
    vmem_spec = pl.BlockSpec(memory_space=pltpu.VMEM)
    return pl.pallas_call(
        kernel,
        out_shape=(
            jax.ShapeDtypeStruct((TOK, FEAT), BF16),
            jax.ShapeDtypeStruct((FEAT, HID), BF16),
            jax.ShapeDtypeStruct((FEAT, HID), BF16),
            jax.ShapeDtypeStruct((HID, FEAT), BF16),
        ),
        in_specs=[vmem_spec, vmem_spec, any_spec, any_spec, any_spec],
        out_specs=(vmem_spec, any_spec, any_spec, any_spec),
        scratch_shapes=[
            vm((2, TOK, FEAT), BF16),
            vm((2, STEPS, 2, SUB, FEAT), BF16),
            vm((FEAT, 2 * HID), BF16),
            vm((HID, FEAT), BF16),
            vm((BLK, H3), F32),
            vm((STEPS, PIECE, H3), F32),
            vm((STEPS, BLK, H3), BF16),
            vm((STEPS, CN - 1, PIECE, H3), BF16),
            vm((STEPS, BLK, H3), BF16),
            vm((STEPS, 2, 2, TOK, FEAT), F32),
            vm((STEPS, 2, TOK, FEAT), F32),
            vm((5, 2, TOK, FEAT), BF16),
            vm((5, 2, TOK, FEAT), BF16),
            vm((ZN - 1, TOK, FEAT), BF16),
            vm((ZN - 1, TOK, FEAT), BF16),
            vm((5, 2, TOK, FEAT), F32),
            vm((FEAT, 2 * HID), BF16),
            vm((HID, FEAT), BF16),
            dma((3,)),
            dma(()),
            dma((3,)),
            dma((3,)),
            dma((3,)),
            dma((7, 2)),
            dma((7, 2)),
            dma((STEPS,)),
            dma((STEPS,)),
            dma((STEPS, CN - 1)),
            dma((STEPS, CN - 1)),
            dma((STEPS, CN - 1)),
            dma((STEPS, CN - 1)),
            dma((STEPS, 2)),
            dma((STEPS, 2)),
            dma((5, 2)),
            dma((5, 2)),
            dma((7,)),
            dma((7,)),
        ],
        compiler_params=pltpu.CompilerParams(
            collective_id=0, has_side_effects=True, vmem_limit_bytes=60 * 2**20
        ),
        cost_estimate=pl.CostEstimate(
            flops=13 * 10**9, bytes_accessed=10**7, transcendentals=5 * 10**4
        ),
        name="swiglu_backward",
    )(tokens, cotangent, w_gate, w_up, w_down)


def solution(mesh):
    placed = (P("row", "col"), P("row", "col"), P("col", "row"), P("col", "row"), P("row", "col"))
    return jax.shard_map(
        local,
        mesh=mesh,
        in_specs=placed,
        out_specs=(P("row", "col"), P("col", "row"), P("col", "row"), P("row", "col")),
        check_vma=False,
    )
```

time: 520 us -> 131 us (0.25)
  the two profiles are of different devices: /device:TPU:98 before, /device:TPU:41 now
where the time goes in v1:
time: 131 us; the launch traced here: 130 us
  Pallas kernels  122 us (93%)
  local copies, waits for them, and re-layouts  7.52 us (6%)
    pallas_call x1, Pallas kernels, local(): pl.pallas_call(kernel, out_shape=(jax.ShapeDtypeStruct((TOK, FEAT), BF16)...  122 us
    unnamed x8, local copies, waits for them, and re-layouts  7.52 us

profile of v1, /device:TPU:41, one launch (start us, length us, event | category | flops | bytes accessed | tf_op | source)
XLA Modules:
  0.0 130.4 jit_solution(13104089107142914208)
XLA Ops:
  0.6 122.2 %swiglu_backward.1 = (bf16[32,2048]{1,0:T(8,128)(2,1)}, bf16[2048,384]{1,0:T(8,128)(2,1)}, bf16[2048,384]{1,0:T(8,128)(2,1)}, bf16[384,2048]{1,0:T(8,128)(2,1)}) custom-call(bf16[32,2048]{1,0:T(8,128)(2,1)} %x_ref.1, bf16[32,2048]{1,0:T(8,128)(2,1)} %dy_ref.1, bf16[2048,384]{1,0:T(8,128)(2,1)} %wg_ref.1, bf16[2048,384]{1,0:T(8,128)(2,1)} %wu_ref.1, ...), custom_call_target="tpu_custom_call" | custom-call | flops 12999999488 | bytes 10000000 | tf_op jit(solution)/shard_map/swiglu_backward/pallas_call | solution.py:257
  122.9 1.6 %copy.13 = bf16[32,2048]{1,0:T(8,128)(2,1)} copy(bf16[32,2048]{1,0:T(8,128)(2,1)} %get-tuple-element.8) | data formatting | bytes 262144
  124.4 0.0 copy-start.1
  124.5 2.8 %copy.14 = bf16[2048,384]{1,0:T(8,128)(2,1)} copy(bf16[2048,384]{1,0:T(8,128)(2,1)} %get-tuple-element.9) | data formatting | bytes 3145728
  127.3 0.0 copy-done.1
  127.3 0.0 copy-start
  127.3 1.1 copy.15
  128.4 0.8 copy-done
  129.3 1.1 copy.16
Async XLA Ops:
  124.4 2.8 %copy-start.1 = (bf16[2048,384]{1,0:T(8,128)(2,1)S(1)}, bf16[2048,384]{1,0:T(8,128)(2,1)}, u32[]{:S(2)}) copy-start(bf16[2048,384]{1,0:T(8,128)(2,1)} %get-tuple-element.10) | copy-start | bytes 4718596
  127.3 2.0 %copy-start = (bf16[384,2048]{1,0:T(8,128)(2,1)S(1)}, bf16[384,2048]{1,0:T(8,128)(2,1)}, u32[]{:S(2)}) copy-start(bf16[384,2048]{1,0:T(8,128)(2,1)} %get-tuple-element.11) | copy-start | bytes 4718596

commit v2 on v1

--- a/solution.py
+++ b/solution.py
@@ -19,6 +19,7 @@
 HID = 384
 H3 = 3 * HID
 TOK = 32
+HALF = FEAT // 2
 
 
 def dot_nn(a, b):
@@ -36,9 +37,9 @@
 def kernel(
     x_ref, dy_ref, wg_ref, wu_ref, wd_ref,
     gt_ref, gwg_ref, gwu_ref, gwd_ref,
-    t_own, xy, wgu, wd, pf, own, pb, rb, hid, gf, r1, s2, r2, s3, rd, acc, ogu, od,
-    w_sem, t_sem, o_sem, ex_s, ex_r, ring_s, ring_r, sib_s, sib_r,
-    b_s, b_r, c_s, c_r, d1_s, d1_r, d2_s, d2_r, d3_s, d3_r,
+    t_own, xy, wgu, wd, pf, own, pb, rb, hid, gf, r1, s2, r2, s3, rd, s4, r4, acc,
+    w_sem, t_sem, ex_s, ex_r, ring_s, ring_r, sib_s, sib_r,
+    b_s, b_r, c_s, c_r, d1_s, d1_r, d2_s, d2_r, d3_s, d3_r, d4_s, d4_r,
 ):
     row = lax.axis_index("row")
     col = lax.axis_index("col")
@@ -49,6 +50,12 @@
 
     def colpeer(r):
         return (row, (col + r) % CN)
+
+    def colat(dx=0, dyl=0):
+        return ((col // 2 + dx) % (CN // 2)) * 2 + (col % 2 + dyl) % 2
+
+    def rows16(q):
+        return pl.ds(pl.multiple_of(q * PIECE, PIECE), PIECE)
 
     sib, partner, cross = at(dc=1), at(dyh=1), at(dyh=1, dc=1)
 
@@ -62,7 +69,7 @@
 
     barrier = pltpu.get_barrier_semaphore()
     greet = [sib, partner, cross]
-    greet += [at(dz=k) for k in range(1, ZN)]
+    greet += [at(dz=k) for k in (1, 2, -2, -1)]
     greet += [colpeer(r) for r in range(1, CN)]
     for d in greet:
         pl.semaphore_signal(barrier, inc=1, device_id=d, device_id_type=MESH)
@@ -156,14 +163,25 @@
         ).astype(BF16)
         hid[s, me16, pl.ds(HID, HID)] = (grad_act * silu).astype(BF16)
         hid[s, me16, pl.ds(2 * HID, HID)] = (silu * up_value).astype(BF16)
-        for r in range(1, CN):
-            go(remote(hid.at[s, me16], hid.at[s, me16], c_s.at[s, r - 1], c_r.at[s, r - 1], colpeer(r)))
+        go(remote(hid.at[s, me16], hid.at[s, me16], c_s.at[s, 0], c_r.at[s, 0], (row, colat(dyl=1))))
+        send_x(s, me16, 0)
+
+    def send_x(s, rows, base):
+        for dx in range(1, CN // 2):
+            q = base + dx
+            go(remote(hid.at[s, rows], hid.at[s, rows], c_s.at[s, q], c_r.at[s, q], (row, colat(dx=dx))))
+
+    def stage_relay(s):
+        piece = rows16(colat(dyl=1))
+        arrived(hid.at[s, piece], hid.at[s, piece], c_s.at[s, 0], c_r.at[s, 0])
+        send_x(s, piece, 3)
 
     def stage_tokens(s):
-        for r in range(1, CN):
-            q = (col - r + CN) % CN
-            piece = hid.at[s, pl.ds(pl.multiple_of(q * PIECE, PIECE), PIECE)]
-            arrived(piece, piece, c_s.at[s, r - 1], c_r.at[s, r - 1])
+        for dx in range(1, CN // 2):
+            for dyl in range(2):
+                piece = hid.at[s, rows16(colat(dx=CN // 2 - dx, dyl=dyl))]
+                q = 3 * dyl + dx
+                arrived(piece, piece, c_s.at[s, q], c_r.at[s, q])
         gf[s] = dot_nt(hid[s, :, : 2 * HID], wgu[...]).reshape(2, 2, TOK, FEAT)
         for d in range(2):
             go(remote(gf.at[s, d, 1 - c], r1.at[s, d], d1_s.at[s, d], d1_r.at[s, d], sib))
@@ -181,72 +199,111 @@
             else:
                 acc[(s + 1) // 2, d] = v
 
+    def hop(slot, dz):
+        go(remote(s3.at[slot], rd.at[slot], d3_s.at[slot], d3_r.at[slot], at(dz=dz)))
+
+    def landed(slot):
+        arrived(rd.at[slot], rd.at[slot], d3_s.at[slot], d3_r.at[slot])
+        return rd[slot].astype(F32)
+
     def stage_home(k):
-        for d in range(2):
-            src = 1 if k in (0, 4) else d
-            if k in (0, 4) and d == 1:
-                continue
-            arrived(r2.at[k, src], r2.at[k, src], d2_s.at[k, src], d2_r.at[k, src])
-            v = acc[k, d] + r2[k, src].astype(F32)
+        if k in (0, 4):
+            arrived(r2.at[k, 1], r2.at[k, 1], d2_s.at[k, 1], d2_r.at[k, 1])
+            v = acc[k, 0] + r2[k, 1].astype(F32)
             if k == 0:
                 acc[0, 0] = v
+                return
+            for d in range(2):
+                s4[d] = v[:, d * HALF : (d + 1) * HALF].astype(BF16)
+                go(remote(s4.at[d], r4.at[d], d4_s.at[d], d4_r.at[d], at(dz=2 if d else -2)))
+            return
+        for d in range(2):
+            arrived(r2.at[k, d], r2.at[k, d], d2_s.at[k, d], d2_r.at[k, d])
+            v = acc[k, d] + r2[k, d].astype(F32)
+            if k == 2:
+                acc[2, d] = v
             else:
-                slot = 2 * (k - 1) + d
+                slot = k - 1 + d
                 s3[slot] = v.astype(BF16)
-                dest = at(dz=k if d else -k)
-                go(remote(s3.at[slot], rd.at[slot], d3_s.at[slot], d3_r.at[slot], dest))
-
-    outs = []
+                hop(slot, 1 if d else -1)
+
+    def stage_join():
+        for d in range(2):
+            acc[2, d] = acc[2, d] + landed(2 + d)
+        for d in range(2):
+            part = pl.ds(d * HALF, HALF)
+            arrived(r4.at[d], r4.at[d], d4_s.at[d], d4_r.at[d])
+            acc[2, d, :, part] = acc[2, d, :, part] + r4[d].astype(F32)
+            s3[4 + d] = acc[2, d].astype(BF16)
+            hop(4 + d, 2 if d else -2)
 
     def weight_grads(which):
         hs = hid[...].reshape(STEPS * BLK, H3)
         if which < 2:
             for m in range(4):
                 f = (which * 4 + m) * 256
-                ogu[pl.ds(f, 256), :] = dot_tn(
+                g = dot_tn(
                     xy[0, :, :, :, f : f + 256].reshape(STEPS * BLK, 256), hs[:, : 2 * HID]
                 ).astype(BF16)
+                gwg_ref[pl.ds(f, 256), :] = g[:, :HID]
+                gwu_ref[pl.ds(f, 256), :] = g[:, HID:]
         else:
             for m in range(8):
                 f = m * 256
-                od[:, pl.ds(f, 256)] = dot_tn(
+                gwd_ref[:, pl.ds(f, 256)] = dot_tn(
                     hs[:, 2 * HID :], xy[1, :, :, :, f : f + 256].reshape(STEPS * BLK, 256)
                 ).astype(BF16)
-        if which == 1:
-            outs.append(pltpu.make_async_copy(ogu.at[:, pl.ds(0, HID)], gwg_ref, o_sem.at[0]))
-            outs.append(pltpu.make_async_copy(ogu.at[:, pl.ds(HID, HID)], gwu_ref, o_sem.at[1]))
-            outs[0].start()
-            outs[1].start()
-        if which == 2:
-            outs.append(pltpu.make_async_copy(od, gwd_ref, o_sem.at[2]))
-            outs[2].start()
-
-    for i in range(STEPS + 4):
+
+    for i in range(STEPS + 5):
         if i < STEPS:
             stage_gather(i)
-        if 0 <= i - 3 < STEPS:
-            stage_pair(i - 3)
+        if 0 <= i - 4 < STEPS:
+            stage_pair(i - 4)
         if i < STEPS:
             stage_forward(i)
         if 0 <= i - 1 < STEPS:
             stage_hidden(i - 1)
         if 0 <= i - 2 < STEPS:
-            stage_tokens(i - 2)
-        j = i - 4
+            stage_relay(i - 2)
+        if 0 <= i - 3 < STEPS:
+            stage_tokens(i - 3)
+        j = i - 5
         if 0 <= j < STEPS and (j % 2 == 0 or j == 7):
             stage_home((j + 1) // 2)
-        if i >= STEPS + 1:
-            weight_grads(i - STEPS - 1)
-
-    total = acc[0, 0]
-    for slot in range(ZN - 1):
-        arrived(rd.at[slot], rd.at[slot], d3_s.at[slot], d3_r.at[slot])
-        total = total + rd[slot].astype(F32)
-    gt_ref[...] = total.astype(BF16)
+        if i == STEPS + 3:
+            weight_grads(0)
+            weight_grads(1)
+
+    stage_join()
+    weight_grads(2)
+    total = acc[0, 0] + landed(0) + landed(1)
+    gt_ref[...] = (total + landed(4) + landed(5)).astype(BF16)
     for cp in pending:
         cp.wait_send()
-    for cp in outs:
+
+
+def store_kernel(a, b, c, d, oa, ob, oc, od, sems):
+    copies = [
+        pltpu.make_async_copy(src, dst, sems.at[i])
+        for i, (src, dst) in enumerate(((a, oa), (b, ob), (c, oc), (d, od)))
+    ]
+    for cp in copies:
+        cp.start()
+    for cp in copies:
         cp.wait()
+
+
+def store(arrays):
+    anywhere = pl.BlockSpec(memory_space=pl.ANY)
+    return pl.pallas_call(
+        store_kernel,
+        out_shape=tuple(jax.ShapeDtypeStruct(a.shape, a.dtype) for a in arrays),
+        in_specs=[anywhere] * 4,
+        out_specs=(anywhere,) * 4,
+        scratch_shapes=[pltpu.SemaphoreType.DMA((4,))],
+        compiler_params=pltpu.CompilerParams(vmem_limit_bytes=2**20),
+        name="store_results",
+    )(*arrays)
 
 
 def local(tokens, cotangent, w_gate, w_up, w_down):
@@ -254,7 +311,7 @@
     vm = pltpu.VMEM
     any_spec = pl.BlockSpec(memory_space=pl.ANY)
     vmem_spec = pl.BlockSpec(memory_space=pltpu.VMEM)
-    return pl.pallas_call(
+    results = pl.pallas_call(
         kernel,
         out_shape=(
             jax.ShapeDtypeStruct((TOK, FEAT), BF16),
@@ -263,7 +320,7 @@
             jax.ShapeDtypeStruct((HID, FEAT), BF16),
         ),
         in_specs=[vmem_spec, vmem_spec, any_spec, any_spec, any_spec],
-        out_specs=(vmem_spec, any_spec, any_spec, any_spec),
+        out_specs=(vmem_spec,) * 4,
         scratch_shapes=[
             vm((2, TOK, FEAT), BF16),
             vm((2, STEPS, 2, SUB, FEAT), BF16),
@@ -278,14 +335,13 @@
             vm((STEPS, 2, TOK, FEAT), F32),
             vm((5, 2, TOK, FEAT), BF16),
             vm((5, 2, TOK, FEAT), BF16),
-            vm((ZN - 1, TOK, FEAT), BF16),
-            vm((ZN - 1, TOK, FEAT), BF16),
+            vm((6, TOK, FEAT), BF16),
+            vm((6, TOK, FEAT), BF16),
+            vm((2, TOK, HALF), BF16),
+            vm((2, TOK, HALF), BF16),
             vm((5, 2, TOK, FEAT), F32),
-            vm((FEAT, 2 * HID), BF16),
-            vm((HID, FEAT), BF16),
             dma((3,)),
             dma(()),
-            dma((3,)),
             dma((3,)),
             dma((3,)),
             dma((7, 2)),
@@ -300,17 +356,20 @@
             dma((STEPS, 2)),
             dma((5, 2)),
             dma((5, 2)),
-            dma((7,)),
-            dma((7,)),
+            dma((6,)),
+            dma((6,)),
+            dma((2,)),
+            dma((2,)),
         ],
         compiler_params=pltpu.CompilerParams(
-            collective_id=0, has_side_effects=True, vmem_limit_bytes=60 * 2**20
+            collective_id=0, has_side_effects=True, vmem_limit_bytes=48 * 2**20
         ),
         cost_estimate=pl.CostEstimate(
             flops=13 * 10**9, bytes_accessed=10**7, transcendentals=5 * 10**4
         ),
         name="swiglu_backward",
     )(tokens, cotangent, w_gate, w_up, w_down)
+    return store(results)
 
 
 def solution(mesh):

time: 131 us -> 112 us (0.85)
  the two profiles are of different devices: /device:TPU:41 before, /device:TPU:9 now
where the time goes in v2:
time: 112 us
  Pallas kernels  109 us (97%)
  local copies, waits for them, and re-layouts  1.8 us (2%)
    pallas_call x1, Pallas kernels, local(): pl.pallas_call(kernel, out_shape=(jax.ShapeDtypeStruct((TOK, FEAT), BF16)...  107 us
    pallas_call x1, Pallas kernels, store(): pl.pallas_call(store_kernel, out_shape=tuple((jax.ShapeDtypeStruct(a.shap...  2.26 us

profile of v2, /device:TPU:9, one launch (start us, length us, event | category | flops | bytes accessed | tf_op | source)
XLA Modules:
  0.0 111.9 jit_solution(7549683497740865932)
XLA Ops:
  0.6 0.0 copy-start
  0.6 0.9 copy-done
  1.5 0.0 copy-start.1
  1.5 0.9 copy-done.1
  2.4 107.0 %swiglu_backward.1 = (bf16[32,2048]{1,0:T(8,128)(2,1)S(1)}, bf16[2048,384]{1,0:T(8,128)(2,1)S(1)}, bf16[2048,384]{1,0:T(8,128)(2,1)S(1)}, bf16[384,2048]{1,0:T(8,128)(2,1)S(1)}) custom-call(bf16[32,2048]{1,0:T(8,128)(2,1)S(1)} %copy-done, bf16[32,2048]{1,0:T(8,128)(2,1)S(1)} %copy-done.1, bf16[2048,384]{1,0:T(8,128)(2,1)} %wg_ref.1, ...), custom_call_target="tpu_custom_call" | custom-call | flops 12999999488 | bytes 10000000 | tf_op jit(solution)/shard_map/swiglu_backward/pallas_call | solution.py:314
  109.5 2.3 %store_results.1 = (bf16[32,2048]{1,0:T(8,128)(2,1)}, bf16[2048,384]{1,0:T(8,128)(2,1)}, bf16[2048,384]{1,0:T(8,128)(2,1)}, bf16[384,2048]{1,0:T(8,128)(2,1)}) custom-call(bf16[32,2048]{1,0:T(8,128)(2,1)S(1)} %get-tuple-element.8.a, bf16[2048,384]{1,0:T(8,128)(2,1)S(1)} %get-tuple-element.9.b, bf16[2048,384]{1,0:T(8,128)(2,1)S(1)} %get-tuple-element.10.c, ...), custom_call_target="tpu_custom_call" | custom-call | tf_op jit(solution)/shard_map/store_results/pallas_call | solution.py:298
Async XLA Ops:
  0.6 0.9 copy-start
  1.5 0.9 copy-start.1

commit v3 on v2

--- a/solution.py
+++ b/solution.py
@@ -254,19 +254,20 @@
                     hs[:, 2 * HID :], xy[1, :, :, :, f : f + 256].reshape(STEPS * BLK, 256)
                 ).astype(BF16)
 
+    stage_gather(0)
     for i in range(STEPS + 5):
-        if i < STEPS:
-            stage_gather(i)
+        if 0 <= i - 0 < STEPS:
+            stage_forward(i - 0)
         if 0 <= i - 4 < STEPS:
             stage_pair(i - 4)
-        if i < STEPS:
-            stage_forward(i)
-        if 0 <= i - 1 < STEPS:
-            stage_hidden(i - 1)
+        if i + 1 < STEPS:
+            stage_gather(i + 1)
         if 0 <= i - 2 < STEPS:
             stage_relay(i - 2)
         if 0 <= i - 3 < STEPS:
             stage_tokens(i - 3)
+        if 0 <= i - 1 < STEPS:
+            stage_hidden(i - 1)
         j = i - 5
         if 0 <= j < STEPS and (j % 2 == 0 or j == 7):
             stage_home((j + 1) // 2)

time: 112 us -> 110 us (0.982)
  the two profiles are of different devices: /device:TPU:9 before, /device:TPU:98 now
where the time goes in v3:
time: 110 us
  Pallas kernels  107 us (97%)
  local copies, waits for them, and re-layouts  1.8 us (2%)
    pallas_call x1, Pallas kernels, local(): pl.pallas_call(kernel, out_shape=(jax.ShapeDtypeStruct((TOK, FEAT), BF16)...  105 us
    pallas_call x1, Pallas kernels, store(): pl.pallas_call(store_kernel, out_shape=tuple((jax.ShapeDtypeStruct(a.shap...  2.26 us

profile of v3, /device:TPU:98, one launch (start us, length us, event | category | flops | bytes accessed | tf_op | source)
XLA Modules:
  0.0 109.6 jit_solution(4714138135237163239)
XLA Ops:
  0.6 0.0 copy-start
  0.6 0.9 copy-done
  1.5 0.0 copy-start.1
  1.5 0.9 copy-done.1
  2.4 104.7 %swiglu_backward.1 = (bf16[32,2048]{1,0:T(8,128)(2,1)S(1)}, bf16[2048,384]{1,0:T(8,128)(2,1)S(1)}, bf16[2048,384]{1,0:T(8,128)(2,1)S(1)}, bf16[384,2048]{1,0:T(8,128)(2,1)S(1)}) custom-call(bf16[32,2048]{1,0:T(8,128)(2,1)S(1)} %copy-done, bf16[32,2048]{1,0:T(8,128)(2,1)S(1)} %copy-done.1, bf16[2048,384]{1,0:T(8,128)(2,1)} %wg_ref.1, ...), custom_call_target="tpu_custom_call" | custom-call | flops 12999999488 | bytes 10000000 | tf_op jit(solution)/shard_map/swiglu_backward/pallas_call | solution.py:315
  107.2 2.3 %store_results.1 = (bf16[32,2048]{1,0:T(8,128)(2,1)}, bf16[2048,384]{1,0:T(8,128)(2,1)}, bf16[2048,384]{1,0:T(8,128)(2,1)}, bf16[384,2048]{1,0:T(8,128)(2,1)}) custom-call(bf16[32,2048]{1,0:T(8,128)(2,1)S(1)} %get-tuple-element.8.a, bf16[2048,384]{1,0:T(8,128)(2,1)S(1)} %get-tuple-element.9.b, bf16[2048,384]{1,0:T(8,128)(2,1)S(1)} %get-tuple-element.10.c, ...), custom_call_target="tpu_custom_call" | custom-call | tf_op jit(solution)/shard_map/store_results/pallas_call | solution.py:299
Async XLA Ops:
  0.6 0.9 copy-start
  1.5 0.9 copy-start.1

commit v4 on v3

--- a/solution.py
+++ b/solution.py
@@ -83,6 +83,10 @@
         )
 
     pending = []
+
+    def sent(keep):
+        while len(pending) > keep:
+            pending.pop(0).wait_send()
 
     def go(cp):
         cp.start()
@@ -274,13 +278,13 @@
         if i == STEPS + 3:
             weight_grads(0)
             weight_grads(1)
+            sent(12)
 
     stage_join()
     weight_grads(2)
     total = acc[0, 0] + landed(0) + landed(1)
     gt_ref[...] = (total + landed(4) + landed(5)).astype(BF16)
-    for cp in pending:
-        cp.wait_send()
+    sent(0)
 
 
 def store_kernel(a, b, c, d, oa, ob, oc, od, sems):

time: 110 us -> 110 us (level)
  no operation moved by 1% of the time
where the time goes in v4:
time: 110 us
  Pallas kernels  107 us (97%)
  local copies, waits for them, and re-layouts  1.8 us (2%)
    pallas_call x1, Pallas kernels, local(): pl.pallas_call(kernel, out_shape=(jax.ShapeDtypeStruct((TOK, FEAT), BF16)...  105 us
    pallas_call x1, Pallas kernels, store(): pl.pallas_call(store_kernel, out_shape=tuple((jax.ShapeDtypeStruct(a.shap...  2.26 us

profile of v4, /device:TPU:98, one launch (start us, length us, event | category | flops | bytes accessed | tf_op | source)
XLA Modules:
  0.0 109.6 jit_solution(2492583786268584066)
XLA Ops:
  0.6 0.0 copy-start
  0.6 0.9 copy-done
  1.5 0.0 copy-start.1
  1.5 0.9 copy-done.1
  2.4 104.7 %swiglu_backward.1 = (bf16[32,2048]{1,0:T(8,128)(2,1)S(1)}, bf16[2048,384]{1,0:T(8,128)(2,1)S(1)}, bf16[2048,384]{1,0:T(8,128)(2,1)S(1)}, bf16[384,2048]{1,0:T(8,128)(2,1)S(1)}) custom-call(bf16[32,2048]{1,0:T(8,128)(2,1)S(1)} %copy-done, bf16[32,2048]{1,0:T(8,128)(2,1)S(1)} %copy-done.1, bf16[2048,384]{1,0:T(8,128)(2,1)} %wg_ref.1, ...), custom_call_target="tpu_custom_call" | custom-call | flops 12999999488 | bytes 10000000 | tf_op jit(solution)/shard_map/swiglu_backward/pallas_call | solution.py:319
  107.2 2.3 %store_results.1 = (bf16[32,2048]{1,0:T(8,128)(2,1)}, bf16[2048,384]{1,0:T(8,128)(2,1)}, bf16[2048,384]{1,0:T(8,128)(2,1)}, bf16[384,2048]{1,0:T(8,128)(2,1)}) custom-call(bf16[32,2048]{1,0:T(8,128)(2,1)S(1)} %get-tuple-element.8.a, bf16[2048,384]{1,0:T(8,128)(2,1)S(1)} %get-tuple-element.9.b, bf16[2048,384]{1,0:T(8,128)(2,1)S(1)} %get-tuple-element.10.c, ...), custom_call_target="tpu_custom_call" | custom-call | tf_op jit(solution)/shard_map/store_results/pallas_call | solution.py:303
Async XLA Ops:
  0.6 0.9 copy-start
  1.5 0.9 copy-start.1
